TPU v7x, 128 devices: a whole 4x4x4 slice. The times are simulated.
128 devices in a mesh: req: 4 (over y), tp: 32 (over x, z, core).
Axes of the slice: x: 4, y: 4, z: 4, core: 2. Of those that a mesh axis runs over, the one named last changes fastest.
Arguments:
- hidden_states: bfloat16 [16, 4, 1024], P('req'), may hold values from -48 to 48
- lengths: int32 [16], P('req'), may hold values from 16 to 4096, as said below
- qkv_weight: bfloat16 [2048, 1024], P('tp'), may hold values from -1 to 1
- rotated_key_cache: bfloat16 [16, 4096, 512], P('req', 'tp'), may hold values from -1000 to 1000
- earlier_value_cache: bfloat16 [16, 4096, 512], P('req', 'tp'), may hold values from -16 to 16
- out_weight: bfloat16 [1024, 1024], P('tp'), may hold values from -0.1875 to 0.1875
- expert_ids: int32 [16, 4, 8], P('req'), may hold values from 0 to 31, all different within a row
- combine_weights: int32 [16, 4, 8], P('req'), may hold values from 4096 to 65535
- gate_up_weight: bfloat16 [32, 1024, 1024], P('tp'), may hold values from -0.1875 to 0.1875
- down_weight: bfloat16 [32, 512, 1024], P('tp'), may hold values from -0.25 to 0.25
Outputs:
- layer_output: bfloat16 [16, 4, 1024], P('req')
Inputs may be any that keep to these rules, and one draw needn't show every extreme that they name: `lengths`: cache length of each request; some request has exactly 4096. `expert_ids`: each token's 8 experts are distinct.
All inputs are finite; a program needn't handle non-finite values.
Results may differ from a plain program's by a relative error of at most 0.008.
Values may be sent and summed in bfloat16 or wider, within the bound.
A program may use at most 64 MiB of HBM per device.

v0:
```python
import jax
import jax.numpy as jnp
from jax import lax
from jax.sharding import PartitionSpec as P

QUERY_HEADS = 16
KEY_VALUE_HEADS = 8
HEAD_DIMENSION = 64


EPSILON = 1e-05
ROPE_BASE = 10000.0
NEGATIVE = -1e30


def merged(part, axis, combine):
    gathered = jax.tree.map(lambda a: lax.all_gather(a, axis), part)

    def take(source):
        return jax.tree.map(lambda a: lax.dynamic_index_in_dim(a, source, 0, False), gathered)

    return lax.fori_loop(
        1, lax.axis_size(axis), lambda source, state: combine(state, take(source)), take(0)
    )


def rms_rows(value_rows):
    return value_rows * lax.rsqrt(
        jnp.mean(value_rows * value_rows, axis=-1, keepdims=True) + EPSILON
    )


def apply_rotation(value_rows, position_index):
    half_width = value_rows.shape[-1] // 2
    rates = ROPE_BASE ** (-2.0 * jnp.arange(half_width, dtype=jnp.float32) / value_rows.shape[-1])
    angles = position_index[:, None, None] * rates
    cosine = jnp.cos(angles)
    sines = jnp.sin(angles)
    front_half = value_rows[..., :half_width]
    back_half = value_rows[..., half_width:]
    return jnp.concatenate(
        [front_half * cosine - back_half * sines, back_half * cosine + front_half * sines], axis=-1
    )


def join_parts(earlier, later):
    highest = jnp.maximum(earlier[0], later[0])
    scale_earlier = jnp.exp(earlier[0] - highest)
    scale_later = jnp.exp(later[0] - highest)
    weight_sum = earlier[1] * scale_earlier + later[1] * scale_later
    value_sum = earlier[2] * scale_earlier[..., None] + later[2] * scale_later[..., None]
    return (highest, weight_sum, value_sum)


def to_columns(value_rows, step_number, group_count):
    request_list, kv_heads, _, head_size = value_rows.shape
    return (
        value_rows.reshape(request_list, kv_heads, step_number, group_count, head_size)
        .transpose(0, 2, 1, 3, 4)
        .reshape(request_list * step_number, kv_heads * group_count * head_size)
    )


def expert_terms(normed, chosen, shares, gate_up_weight, down_weight, first_expert):
    ff_width = down_weight.shape[1]
    united_out = jnp.einsum(
        "nd,edf->enf", normed, gate_up_weight, preferred_element_type=jnp.float32
    )
    activation = (jax.nn.silu(united_out[..., :ff_width]) * united_out[..., ff_width:]).astype(
        jnp.bfloat16
    )
    outcome = jnp.einsum(
        "enf,efd->end", activation, down_weight, preferred_element_type=jnp.float32
    )
    owners = first_expert + jnp.arange(gate_up_weight.shape[0], dtype=jnp.int32)
    factors = jnp.sum(
        jnp.where(chosen[None, :, :] == owners[:, None, None], shares[None, :, :], 0.0), axis=-1
    )
    return jnp.sum(factors[:, :, None] * outcome, axis=0)


def per_device(
    hidden_states,
    lengths,
    qkv_weight,
    rotated_key_cache,
    earlier_value_cache,
    out_weight,
    expert_ids,
    combine_weights,
    gate_up_weight,
    down_weight,
):
    request_list, step_number, model_width = hidden_states.shape
    token_rows = request_list * step_number
    group_count = QUERY_HEADS // KEY_VALUE_HEADS
    query_total_width = QUERY_HEADS * HEAD_DIMENSION
    key_value_width = KEY_VALUE_HEADS * HEAD_DIMENSION
    score_scale = HEAD_DIMENSION ** (-0.5)
    inputs_flat = hidden_states.reshape(token_rows, model_width)
    normed = rms_rows(inputs_flat.astype(jnp.float32)).astype(jnp.bfloat16)
    projected_part = lax.dot_general(
        qkv_weight, normed, (((1,), (1,)), ((), ())), preferred_element_type=jnp.float32
    ).astype(jnp.bfloat16)
    projected_all = lax.all_gather(projected_part, "tp", axis=0, tiled=True)
    query_key_value_rows = projected_all.T
    position_index = (
        (lengths[:, None] + jnp.arange(step_number, dtype=jnp.int32)[None, :])
        .reshape(token_rows)
        .astype(jnp.float32)
    )
    query_rows = apply_rotation(
        query_key_value_rows[:, :query_total_width]
        .reshape(token_rows, QUERY_HEADS, HEAD_DIMENSION)
        .astype(jnp.float32),
        position_index,
    ).astype(jnp.bfloat16)
    fresh_keys = apply_rotation(
        query_key_value_rows[:, query_total_width : query_total_width + key_value_width]
        .reshape(token_rows, KEY_VALUE_HEADS, HEAD_DIMENSION)
        .astype(jnp.float32),
        position_index,
    ).astype(jnp.bfloat16)
    fresh_values = query_key_value_rows[:, query_total_width + key_value_width :].reshape(
        request_list, step_number, KEY_VALUE_HEADS, HEAD_DIMENSION
    )
    grouped_rows = (
        query_rows.reshape(request_list, step_number, KEY_VALUE_HEADS, group_count, HEAD_DIMENSION)
        .transpose(0, 2, 1, 3, 4)
        .reshape(request_list, KEY_VALUE_HEADS, step_number * group_count, HEAD_DIMENSION)
    )
    cache_extent = rotated_key_cache.shape[1]
    stored_keys = rotated_key_cache.reshape(
        request_list, cache_extent, KEY_VALUE_HEADS, HEAD_DIMENSION
    )
    stored_values = earlier_value_cache.reshape(
        request_list, cache_extent, KEY_VALUE_HEADS, HEAD_DIMENSION
    )
    scores = (
        jnp.einsum("bgqd,bcgd->bgqc", grouped_rows, stored_keys, preferred_element_type=jnp.float32)
        * score_scale
    )
    start_pos = lax.axis_index("tp") * cache_extent
    live_rows = (start_pos + jnp.arange(cache_extent, dtype=jnp.int32))[None, :] < lengths[:, None]
    live_mask = live_rows[:, None, None, :]
    masked = jnp.where(live_mask, scores, NEGATIVE)
    highest = jnp.max(masked, axis=-1)
    weights = jnp.where(live_mask, jnp.exp(masked - highest[..., None]), 0.0)
    weight_sum = jnp.sum(weights, axis=-1)
    value_sum = jnp.einsum(
        "bgqc,bcgd->bgqd",
        weights.astype(jnp.bfloat16),
        stored_values,
        preferred_element_type=jnp.float32,
    )
    feature_rows = out_weight.shape[0]
    column_begin = lax.axis_index("tp") * feature_rows
    top_score, total_all, sum_all = merged((highest, weight_sum, value_sum), "tp", join_parts)
    grouped_keys = fresh_keys.reshape(request_list, step_number, KEY_VALUE_HEADS, HEAD_DIMENSION)
    new_scores = (
        jnp.einsum(
            "bgqd,bsgd->bgqs", grouped_rows, grouped_keys, preferred_element_type=jnp.float32
        )
        * score_scale
    )
    query_step = jnp.arange(step_number * group_count, dtype=jnp.int32) // group_count
    causal = jnp.arange(step_number, dtype=jnp.int32)[None, :] <= query_step[:, None]
    new_masked = jnp.where(causal, new_scores, NEGATIVE)
    final_peak = jnp.maximum(top_score, jnp.max(new_masked, axis=-1))
    new_weights = jnp.where(causal, jnp.exp(new_masked - final_peak[..., None]), 0.0)
    carried = jnp.exp(top_score - final_peak)
    denominator = total_all * carried + jnp.sum(new_weights, axis=-1)
    new_part = jnp.einsum(
        "bgqs,bsgd->bgqd",
        new_weights.astype(jnp.bfloat16),
        fresh_values,
        preferred_element_type=jnp.float32,
    )
    numerator = sum_all * carried[..., None] + new_part
    attended = to_columns(numerator / denominator[..., None], step_number, group_count).astype(
        jnp.bfloat16
    )
    attended_part = lax.dynamic_slice_in_dim(attended, column_begin, feature_rows, 1)
    first_expert = lax.axis_index("tp") * gate_up_weight.shape[0]
    chosen = expert_ids.reshape(token_rows, -1)
    shares = combine_weights.reshape(token_rows, -1).astype(jnp.float32) / 65536.0
    head_terms = jnp.dot(attended_part, out_weight, preferred_element_type=jnp.float32)
    projected_rows = lax.psum(head_terms, "tp")
    residual = inputs_flat.astype(jnp.float32) + projected_rows
    normed_second = rms_rows(residual).astype(jnp.bfloat16)
    mixture = lax.psum(
        expert_terms(
            normed_second, chosen, shares, gate_up_weight, down_weight, first_expert
        ).astype(jnp.bfloat16),
        "tp",
    ).astype(jnp.float32)
    final_result = (residual + mixture).astype(jnp.bfloat16)
    return final_result.reshape(request_list, step_number, model_width)


def solution(mesh):
    in_specs = (
        P("req", None, None),
        P("req"),
        P("tp", None),
        P("req", "tp", None),
        P("req", "tp", None),
        P("tp", None),
        P("req", None, None),
        P("req", None, None),
        P("tp", None, None),
        P("tp", None, None),
    )
    out_specs = P("req", None, None)
    return jax.shard_map(
        per_device, mesh=mesh, in_specs=in_specs, out_specs=out_specs, check_vma=False
    )
```

profile of v0, /device:TPU:1, one launch (start us, length us, event | category | flops | bytes accessed | tf_op | source)
XLA Modules:
  0.0 354.1 jit_solution(16797033778908578031)
XLA Ops:
  10.0 1.1 fusion.13
  11.1 27.2 %all-gather.3 = bf16[32,64,16]{1,2,0:T(8,128)(2,1)S(1)} all-gather(bf16[1,64,16]{1,2,0:T(8,128)(2,1)S(1)} %fusion.13), channel_id=1, replica_groups=mesh['req'=4,'tp'=32] {'tp'}, dimensions={0}, use_global_device_ids=true | all-gather | bytes 67584 | tf_op jit(solution)/shard_map/all_gather | solution.py:105
  39.4 1.3 copy.24
  41.1 1.1 fusion.17
  44.0 24.2 %all-gather.1 = f32[128,8,8]{2,1,0:T(8,128)S(1)} all-gather(f32[4,8,8]{2,1,0:T(8,128)S(1)} %fusion.16), channel_id=3, replica_groups=mesh['req'=4,'tp'=32] {'tp'}, dimensions={0}, use_global_device_ids=true | all-gather | bytes 33792 | tf_op jit(solution)/shard_map/all_gather | solution.py:17
  68.2 22.6 %all-gather = f32[128,8,8]{2,1,0:T(8,128)S(1)} all-gather(f32[4,8,8]{2,1,0:T(8,128)S(1)} %get-tuple-element.216), channel_id=2, replica_groups=mesh['req'=4,'tp'=32] {'tp'}, dimensions={0}, use_global_device_ids=true | all-gather | bytes 33792 | tf_op jit(solution)/shard_map/all_gather | solution.py:17
  92.8 34.9 %while.19 = (s32[]{:T(128)}, f32[4,8,8]{2,1,0:T(8,128)S(1)}, f32[4,8,8]{2,1,0:T(8,128)S(1)}, f32[4,8,8,64]{3,2,1,0:T(8,128)S(1)}, f32[32,4,8,8]{3,2,1,0:T(8,128)...) while((s32[]{:T(128)}, f32[4,8,8]{2,1,0:T(8,128)S(1)}, ...), condition=%wide.region_4.5_spmd, body=%wide.region_3.4_spmd.sunk | while | flops 50693 | bytes 206991 | solution.py:22
  92.9 1.1 fusion.57
  94.0 1.1 fusion.57
  95.1 1.1 fusion.57
  96.2 1.1 fusion.57
  97.4 1.1 fusion.57
  98.5 1.1 fusion.57
  99.6 1.1 fusion.57
  100.7 1.1 fusion.57
  101.9 1.1 fusion.57
  104.1 1.1 fusion.57
  105.3 1.1 fusion.57
  106.4 1.1 fusion.57
  107.5 1.1 fusion.57
  108.6 1.1 fusion.57
  109.8 1.1 fusion.57
  131.3 93.6 %all-reduce.2.cloned.1.call-done = f32[16,1024]{1,0:T(8,128)} async-done(((f32[16,1024]{1,0:T(8,128)}), f32[16,1024]{1,0:T(8,128)}) %all-reduce.2.cloned.1.call-update) | async-done | bytes 65552 | tf_op jit(solution)/shard_map/psum | solution.py:188
  226.6 120.1 %psum.15 = bf16[16,1024]{1,0:T(8,128)(2,1)S(1)} all-reduce(bf16[16,1024]{1,0:T(8,128)(2,1)S(1)} %fusion.12), channel_id=1, replica_groups=mesh['req'=4,'tp'=32] {'tp'}, use_global_device_ids=true, to_apply=%region_10.11 | all-reduce | flops 16384 | bytes 65536 | tf_op jit(solution)/shard_map/psum | solution.py:191
  (109 shorter events, 32.2 us)
Async XLA Ops:
  6.5 219.4 %copy-start = (bf16[1,1024,1024]{2,1,0:T(8,128)(2,1)S(1)}, bf16[1,1024,1024]{2,1,0:T(8,128)(2,1)}, u32[]{:S(2)}) copy-start(bf16[1,1024,1024]{2,1,0:T(8,128)(2,1)} %param.20) | copy-start | bytes 6291460
  6.5 32.6 %copy-start.2 = (bf16[4,128,512]{2,1,0:T(8,128)(2,1)S(1)}, bf16[4,128,512]{2,1,0:T(8,128)(2,1)}, u32[]{:S(2)}) copy-start(bf16[4,128,512]{2,1,0:T(8,128)(2,1)} %param.15) | copy-start | bytes 1572868
  6.5 85.3 %all-gather.6.cloned.1.call-start = ((), (), s32[]{:S(2)}) async-start(), calls=%async_computation.1 | async-start | bytes 4325376 | tf_op jit(solution)/shard_map/all_gather | solution.py:17
  42.2 182.7 %all-reduce.2.cloned.1.call-start = ((), (), s32[]{:S(2)}) async-start(), calls=%async_computation | async-start | bytes 131072 | tf_op jit(solution)/shard_map/psum | solution.py:188
  90.8 1.1 copy-start.4
  92.8 36.8 %copy-start.3 = (bf16[32,1024]{1,0:T(8,128)(2,1)S(1)}, bf16[32,1024]{1,0:T(8,128)(2,1)}, u32[]{:S(2)}) copy-start(bf16[32,1024]{1,0:T(8,128)(2,1)} %param.17) | copy-start | bytes 196612
  127.8 98.6 %copy-start.1 = (bf16[1,512,1024]{2,1,0:T(8,128)(2,1)S(1)}, bf16[1,512,1024]{2,1,0:T(8,128)(2,1)}, u32[]{:S(2)}) copy-start(bf16[1,512,1024]{2,1,0:T(8,128)(2,1)} %param.21) | copy-start | bytes 3145732
Sparse Core Ops, SparseCore 0:
  42.3 45.6 all-gather.5
  130.5 94.3 all-reduce.1
where the time goes:
time: 359 us; the launch traced here: 354 us
  blocking collectives  194 us (54%)
  waiting for transfers between devices  93.7 us (26%)
  other arithmetic  39.8 us (11%)
  between operations  13.6 us (4%)
  local copies, waits for them, and re-layouts  6.09 us (2%)
  matrix products  5.89 us (2%)
    psum x1, blocking collectives, per_device(): lax.psum(expert_terms(normed_second, chosen, shares, gate_up_weight, down...  120 us
    psum x1, waiting for transfers between devices, per_device(): projected_rows = lax.psum(head_terms, 'tp')  93.6 us
    all_gather x2, blocking collectives, merged(): gathered = jax.tree.map(lambda a: lax.all_gather(a, axis), part)  46.8 us
    add x31, other arithmetic, join_parts(): earlier[2] * scale_earlier[..., None] + later[2] * scale_later[..., None]  33.3 us
    all_gather x1, blocking collectives, per_device(): projected_all = lax.all_gather(projected_part, 'tp', axis=0, tiled=True)  27.2 us
  transfers between devices with their start and end apart: 2, of which 1 were waited for; matrix products, arithmetic and copies ran while one was open for 1% of the time, Pallas kernels for 0%

commit v1 on v0

v1 whole, which is shorter than its diff:
```python
import functools

import jax
import jax.numpy as jnp
import numpy as np
from jax import lax
from jax.experimental import pallas as pl
from jax.experimental.pallas import tpu as pltpu
from jax.sharding import PartitionSpec as P

EPSILON = 1e-05
ROPE_BASE = 10000.0
NEGATIVE = -1e30
MESH = pl.DeviceIdType.MESH
F32 = jnp.float32
BF16 = jnp.bfloat16


def hops(offset):
    return min(offset, 4 - offset)


PEERS = sorted(
    [(dx, dz, dc) for dx in range(4) for dz in range(4) for dc in range(2) if dx or dz or dc],
    key=lambda o: -(hops(o[0]) + hops(o[1]) + 0.5 * o[2]),
)


def stack_rows(pieces):
    return jnp.concatenate(pieces, axis=0)


def kernel(
    hidden_h, lengths_h, qkv_h, keys_h, values_h, outw_h, ids_h, comb_h, gate_h, down_h, rates_h,
    out_h,
    hidden_v, lengths_s, qkv_v, keys_v, values_v, ids_v, comb_v, gate_v, down_v, rates_v,
    qsend, qbuf, wbuf, asend, abuf, psend, pbuf, rsend, rbuf, msend, mbuf, osend,
    lsem, ssem, rsem,
):
    me = lax.axis_index("tp")
    x = lax.div(me, 8)
    z = lax.rem(lax.div(me, 2), 4)
    c = lax.rem(me, 2)
    g_me = 2 * x + c

    def device(offset):
        dx, dz, dc = offset
        px = lax.rem(x + dx, 4) if dx else x
        pz = lax.rem(z + dz, 4) if dz else z
        pc = lax.rem(c + dc, 2) if dc else c
        return px, pz, pc

    def index(offset):
        px, pz, pc = device(offset)
        return px * 8 + pz * 2 + pc

    peers = [index(o) for o in PEERS]

    barrier = pltpu.get_barrier_semaphore()
    for p in peers:
        pl.semaphore_signal(barrier, inc=1, device_id={"tp": p}, device_id_type=MESH)

    def load(src, dst, i):
        copy = pltpu.make_async_copy(src, dst, lsem.at[i])
        copy.start()
        return copy

    c_hidden = load(hidden_h, hidden_v, 0)
    c_len = load(lengths_h, lengths_s, 1)
    c_qkv0 = load(qkv_h, qkv_v.at[pl.ds(0, 64)], 2)
    c_qkv1 = load(qkv_h, qkv_v.at[pl.ds(64, 64)], 3)
    c_rates = load(rates_h, rates_v, 4)
    c_keys = load(keys_h, keys_v, 5)
    c_values = load(values_h, values_v, 6)
    c_ids = load(ids_h, ids_v, 7)
    c_comb = load(comb_h, comb_v, 8)
    c_gate = load(gate_h.at[0], gate_v, 9)
    c_down = load(down_h.at[0], down_v, 10)

    def send(src, dst, phase, p):
        pltpu.make_async_remote_copy(
            src_ref=src, dst_ref=dst, send_sem=ssem.at[phase], recv_sem=rsem.at[phase],
            device_id={"tp": p}, device_id_type=MESH,
        ).start()

    def wait_bytes(ref, sem):
        pltpu.make_async_copy(ref, ref, sem).wait()

    sub = lax.broadcasted_iota(jnp.int32, (8, 128), 0)
    lane = lax.broadcasted_iota(jnp.int32, (8, 128), 1)
    low_half = lane < 64
    top_rows = sub < 4

    c_hidden.wait()
    rows = stack_rows([hidden_v[r].astype(F32) for r in range(4)])
    normed = (
        rows * lax.rsqrt(jnp.mean(rows * rows, axis=-1, keepdims=True) + EPSILON)
    ).astype(BF16)
    c_len.wait()
    lens = [lengths_s[r] for r in range(4)]
    c_rates.wait()
    front = jnp.where(top_rows, lens[0], lens[1])
    rear = jnp.where(top_rows, lens[2], lens[3])
    position = (jnp.where(low_half, front, rear) + jnp.bitwise_and(sub, 3)).astype(F32)
    angles = position * rates_v[...]
    cosine = jnp.cos(angles)
    sine = jnp.sin(angles)
    c_qkv0.wait()
    c_qkv1.wait()
    head = lax.dot_general(
        normed, qkv_v[...], (((1,), (1,)), ((), ())), preferred_element_type=F32
    )
    head = head.astype(BF16).astype(F32)
    packed = jnp.where(low_half, head[0:8], head[8:16])
    ahead = pltpu.roll(packed, 96, 1)
    behind = pltpu.roll(packed, 32, 1)
    first = jnp.bitwise_and(lane, 63) < 32
    turned = packed * cosine + jnp.where(first, -ahead, behind) * sine
    scale = jnp.where(me < 16, 0.125, 1.0).astype(F32)
    rotated = jnp.broadcast_to(me, (8, 128)) < 24
    qsend[...] = jnp.where(rotated, turned.astype(BF16).astype(F32) * scale, packed).astype(BF16)

    pl.semaphore_wait(barrier, 31)
    for p in peers:
        send(qsend, qbuf.at[me], 0, p)
    pltpu.make_async_copy(qsend, qbuf.at[me], rsem.at[0]).start()

    slot = 2 * lax.rem(z, 2) + c
    owner_core = lax.div(z, 2)
    for dz in (2, 1, 3):
        send(outw_h, wbuf.at[slot], 1, x * 8 + lax.rem(z + dz, 4) * 2 + owner_core)

    @pl.when(owner_core == c)
    def _():
        pltpu.make_async_copy(outw_h, wbuf.at[slot], rsem.at[1]).start()

    @pl.when(owner_core != c)
    def _():
        send(outw_h, wbuf.at[slot], 1, x * 8 + z * 2 + owner_core)

    wait_bytes(qbuf, rsem.at[0])
    heads = [qbuf[h].astype(F32) for h in range(16)]
    mixed = []
    for g in range(8):
        e, f = heads[2 * g], heads[2 * g + 1]
        mixed.append(
            (
                jnp.where(top_rows, e, pltpu.roll(f, 4, 0)),
                jnp.where(top_rows, pltpu.roll(e, 4, 0), f),
            )
        )
    c_keys.wait()
    c_values.wait()
    zero = jnp.zeros((8, 128), F32)
    cell = lax.broadcasted_iota(jnp.int32, (64, 128), 1) + me * 128
    for r in range(4):
        blocks = []
        for g in range(8):
            u = mixed[g][r % 2]
            if r // 2 != g % 2:
                u = pltpu.roll(u, 64, 1)
            blocks.append(jnp.where(low_half if g % 2 == 0 else ~low_half, u, 0.0))
        columns = [
            jnp.concatenate([blocks[g] if g // 2 == k else zero for g in range(8)], axis=0)
            for k in range(4)
        ]
        queries = jnp.concatenate(columns, axis=1).astype(BF16)
        scores = lax.dot_general(
            queries, keys_v[r], (((1,), (1,)), ((), ())), preferred_element_type=F32
        )
        live = cell < lens[r]
        masked = jnp.where(live, scores, NEGATIVE)
        peak = jnp.max(masked, axis=-1, keepdims=True)
        weights = jnp.where(live, jnp.exp(masked - peak), 0.0)
        total = jnp.sum(weights, axis=-1, keepdims=True)
        sums = jnp.dot(weights.astype(BF16), values_v[r], preferred_element_type=F32)
        for g in range(8):
            o = sums[8 * g : 8 * g + 8, (g // 2) * 128 : (g // 2) * 128 + 128]
            if g % 2:
                o = pltpu.roll(o, 64, 1)
            stats = jnp.where(
                lane < 96,
                jnp.broadcast_to(peak[8 * g : 8 * g + 8], (8, 128)),
                jnp.broadcast_to(total[8 * g : 8 * g + 8], (8, 128)),
            )
            asend[(g // 2) * 8 + r * 2 + g % 2] = jnp.where(low_half, o, stats)

    for p in peers:
        send(asend.at[p], abuf.at[me], 2, p)
    pltpu.make_async_copy(asend.at[me], abuf.at[me], rsem.at[2]).start()

    late = jnp.broadcast_to(lax.rem(z, 2), (8, 128)) == 1
    rear_half = jnp.broadcast_to(lax.div(z, 2), (8, 128)) == 1
    e = qbuf[2 * g_me].astype(F32)
    f = qbuf[2 * g_me + 1].astype(F32)
    u = jnp.where(
        late,
        jnp.where(top_rows, pltpu.roll(e, 4, 0), f),
        jnp.where(top_rows, e, pltpu.roll(f, 4, 0)),
    )
    own_queries = jnp.where(low_half, jnp.where(rear_half, pltpu.roll(u, 64, 1), u), 0.0)

    def own_rows(i):
        v = qbuf[i].astype(F32)
        v = jnp.where(rear_half, pltpu.roll(v, 64, 1), v)
        return jnp.where(late, pltpu.roll(v, 4, 0), v)

    new_keys = own_rows(16 + g_me)
    new_values = own_rows(24 + g_me)
    step = jnp.bitwise_and(sub, 3)
    new_scores = []
    for s in range(4):
        score = jnp.sum(
            own_queries * jnp.broadcast_to(new_keys[s : s + 1], (8, 128)), axis=-1, keepdims=True
        )
        new_scores.append(
            jnp.where(step >= s, jnp.broadcast_to(score, (8, 128)), NEGATIVE)
        )
    new_peak = functools.reduce(jnp.maximum, new_scores)
    new_weights = [jnp.exp(v - new_peak) for v in new_scores]
    new_total = functools.reduce(jnp.add, new_weights)
    new_sum = functools.reduce(
        jnp.add,
        [
            new_weights[s].astype(BF16).astype(F32)
            * jnp.broadcast_to(new_values[s : s + 1], (8, 128))
            for s in range(4)
        ],
    )
    c_ids.wait()
    c_comb.wait()
    factors = [
        jnp.sum(
            jnp.where(ids_v[r] == me, comb_v[r], 0).astype(F32), axis=-1, keepdims=True
        )
        * (1.0 / 65536.0)
        for r in range(4)
    ]
    wait_bytes(wbuf, rsem.at[1])

    wait_bytes(abuf, rsem.at[2])
    peaks = [jnp.broadcast_to(abuf[b][:, 64:65], (8, 128)) for b in range(32)]
    top = functools.reduce(jnp.maximum, peaks + [new_peak])
    total_all = jnp.zeros((8, 128), F32)
    for b in range(32):
        total_all = total_all + jnp.exp(peaks[b] - top) * abuf[b]
    carried = jnp.exp(new_peak - top)
    denominator = jnp.broadcast_to(total_all[:, 96:97], (8, 128)) + carried * new_total
    attended = jnp.where(low_half, (total_all + carried * new_sum) / denominator, 0.0)
    attended = jnp.where(top_rows, attended, pltpu.roll(attended, 64, 1)).astype(BF16)
    product = jnp.dot(
        attended, wbuf[...].reshape(128, 1024), preferred_element_type=F32
    )
    product = product[0:4] + product[4:8]
    for k in range(8):
        psend[k] = product[:, k * 128 : k * 128 + 128]
    row_peers = [o for o in PEERS if o[1] == 0]
    for o in row_peers:
        px, _, pc = device(o)
        send(psend.at[2 * px + pc], pbuf.at[g_me], 3, index(o))
    pltpu.make_async_copy(psend.at[g_me], pbuf.at[g_me], rsem.at[3]).start()

    own_column = pl.multiple_of(g_me * 128, 128)
    own_hidden = hidden_v[z, :, pl.ds(own_column, 128)].astype(F32)
    wait_bytes(pbuf, rsem.at[3])
    residual = own_hidden + jnp.sum(pbuf[...], axis=0)
    rsend[...] = residual
    for p in peers:
        send(rsend, rbuf.at[g_me, z], 4, p)
    pltpu.make_async_copy(rsend, rbuf.at[g_me, z], rsem.at[4]).start()
    c_gate.wait()
    c_down.wait()
    wait_bytes(rbuf, rsem.at[4])
    rows = jnp.concatenate(
        [stack_rows([rbuf[k, r] for r in range(4)]) for k in range(8)], axis=1
    )
    normed = (
        rows * lax.rsqrt(jnp.mean(rows * rows, axis=-1, keepdims=True) + EPSILON)
    ).astype(BF16)
    united = jnp.dot(normed, gate_v[...], preferred_element_type=F32)
    gate = united[:, :512]
    activation = (gate / (1.0 + jnp.exp(-gate)) * united[:, 512:]).astype(BF16)
    outcome = jnp.dot(activation, down_v[...], preferred_element_type=F32)
    for r in range(4):
        share = outcome[4 * r : 4 * r + 4] * factors[r]
        for g in range(8):
            msend[(g // 2) * 8 + r * 2 + g % 2] = share[:, g * 128 : g * 128 + 128].astype(BF16)
    for p in peers:
        send(msend.at[p], mbuf.at[me], 5, p)
    pltpu.make_async_copy(msend.at[me], mbuf.at[me], rsem.at[5]).start()
    wait_bytes(mbuf, rsem.at[5])
    osend[...] = (residual + jnp.sum(mbuf[...].astype(F32), axis=0)).astype(BF16)
    target = out_h.at[z, :, pl.ds(own_column, 128)]
    for p in peers:
        send(osend, target, 6, p)
    pltpu.make_async_copy(osend, target, rsem.at[6]).start()
    wait_bytes(out_h, rsem.at[6])

    wait_bytes(qbuf.at[pl.ds(0, 31)], ssem.at[0])
    wait_bytes(wbuf.at[pl.ds(0, 3)], ssem.at[1])

    @pl.when(owner_core != c)
    def _():
        wait_bytes(wbuf.at[0], ssem.at[1])

    wait_bytes(abuf.at[pl.ds(0, 31)], ssem.at[2])
    wait_bytes(pbuf.at[pl.ds(0, 7)], ssem.at[3])
    wait_bytes(qbuf.at[pl.ds(0, 31)], ssem.at[4])
    wait_bytes(mbuf.at[pl.ds(0, 31)], ssem.at[5])
    wait_bytes(mbuf.at[pl.ds(0, 31)], ssem.at[6])


def per_device(*args):
    half = np.arange(128) % 32
    rates = np.broadcast_to(
        (ROPE_BASE ** (-2.0 * half / 64.0)).astype(np.float32)[None, :], (8, 128)
    )
    anywhere = pl.BlockSpec(memory_space=pl.ANY)
    return pl.pallas_call(
        kernel,
        out_shape=jax.ShapeDtypeStruct((4, 4, 1024), BF16),
        in_specs=[anywhere] * 11,
        out_specs=anywhere,
        scratch_shapes=[
            pltpu.VMEM((4, 4, 1024), BF16),
            pltpu.SMEM((4,), jnp.int32),
            pltpu.VMEM((128, 1024), BF16),
            pltpu.VMEM((4, 128, 512), BF16),
            pltpu.VMEM((4, 128, 512), BF16),
            pltpu.VMEM((4, 4, 8), jnp.int32),
            pltpu.VMEM((4, 4, 8), jnp.int32),
            pltpu.VMEM((1024, 1024), BF16),
            pltpu.VMEM((512, 1024), BF16),
            pltpu.VMEM((8, 128), F32),
            pltpu.VMEM((8, 128), BF16),
            pltpu.VMEM((32, 8, 128), BF16),
            pltpu.VMEM((4, 32, 1024), BF16),
            pltpu.VMEM((32, 8, 128), F32),
            pltpu.VMEM((32, 8, 128), F32),
            pltpu.VMEM((8, 4, 128), F32),
            pltpu.VMEM((8, 4, 128), F32),
            pltpu.VMEM((4, 128), F32),
            pltpu.VMEM((8, 4, 4, 128), F32),
            pltpu.VMEM((32, 4, 128), BF16),
            pltpu.VMEM((32, 4, 128), BF16),
            pltpu.VMEM((4, 128), BF16),
            pltpu.SemaphoreType.DMA((11,)),
            pltpu.SemaphoreType.DMA((7,)),
            pltpu.SemaphoreType.DMA((7,)),
        ],
        compiler_params=pltpu.CompilerParams(collective_id=0, has_side_effects=True),
        name="decoder_layer",
    )(*args, jnp.asarray(rates))


def solution(mesh):
    in_specs = (
        P("req", None, None),
        P("req"),
        P("tp", None),
        P("req", "tp", None),
        P("req", "tp", None),
        P("tp", None),
        P("req", None, None),
        P("req", None, None),
        P("tp", None, None),
        P("tp", None, None),
    )
    out_specs = P("req", None, None)
    return jax.shard_map(
        per_device, mesh=mesh, in_specs=in_specs, out_specs=out_specs, check_vma=False
    )
```

time: 359 us -> 39.2 us (0.11); the launches traced: 354 us -> 39 us
  blocking collectives: 194 us -> 0 us
  waiting for transfers between devices: 93.7 us -> 0 us
  other arithmetic: 39.8 us -> 0 us
  Pallas kernels: 0 us -> 36.4 us
  between operations: 13.6 us -> 0.01 us
  matrix products: 5.89 us -> 0 us
    psum x1 -> x0, blocking collectives: 120 us -> none  [per_device(): lax.psum(expert_terms(normed_second, chosen, shares, gate_up_weight, down...]
    psum x1 -> x0, waiting for transfers between devices: 93.6 us -> none  [per_device(): projected_rows = lax.psum(head_terms, 'tp')]
    all_gather x3 -> x0, blocking collectives: 74 us -> none  [the longest x2 46.8 us: merged(): gathered = jax.tree.map(lambda a: lax.all_gather(a, axis), part)]
    pallas_call x0 -> x1, Pallas kernels: none -> 36.4 us  [per_device(): pl.pallas_call(kernel, out_shape=jax.ShapeDtypeStruct((4, 4, 1024), BF16)...]
    add x64 -> x0, other arithmetic: 34 us -> none  [the longest x31 33.3 us: join_parts(): earlier[2] * scale_earlier[..., None] + later[2] * scale_later[..., None]]
    dot_general x8 -> x0, matrix products: 5.89 us -> none  [the longest x1 1.1 us: per_device(): lax.dot_general(qkv_weight, normed, (((1,), (1,)), ((), ())), preferred_e...]
    reduce_sum x5 -> x0, other arithmetic: 3.75 us -> none  [the longest x2 1.99 us: rms_rows(): jnp.mean(value_rows * value_rows, axis=-1, keepdims=True) + EPSILON]
  transfers between devices with their start and end apart: 2 -> 0, of which waited for: 1 -> 0; matrix products, arithmetic and copies ran while one was open for 1% -> 0% of each run, Pallas kernels for 0% -> 0%
where the time goes in v1:
time: 39.2 us; the launch traced here: 39 us
  Pallas kernels  36.4 us (93%)
  local copies, waits for them, and re-layouts  2.63 us (7%)
    pallas_call x1, Pallas kernels, per_device(): pl.pallas_call(kernel, out_shape=jax.ShapeDtypeStruct((4, 4, 1024), BF16)...  36.4 us
    unnamed x1, local copies, waits for them, and re-layouts  1.39 us
    another operation x1, local copies, waits for them, and re-layouts  1.25 us

profile of v1, /device:TPU:1, one launch (start us, length us, event | category | flops | bytes accessed | tf_op | source)
XLA Modules:
  0.0 39.0 jit_solution(16668193330422339171)
XLA Ops:
  0.0 1.2 %jit_solution_.3.rates_h = f32[8,128]{1,0:T(8,128)} broadcast(f32[128]{0:T(128)} %constant.2.clone), dimensions={1} | broadcast | bytes 4608 | tf_op jit(solution)
  1.2 36.4 %decoder_layer.1 = bf16[4,4,1024]{2,1,0:T(4,128)(2,1)} custom-call(bf16[4,4,1024]{2,1,0:T(4,128)(2,1)} %hidden_h.1, s32[4]{0:T(128)} %lengths_h.1, bf16[64,1024]{1,0:T(8,128)(2,1)} %qkv_h.1, bf16[4,128,512]{2,1,0:T(8,128)(2,1)} %keys_h.1, bf16[4,128,512]{2,1,0:T(8,128)(2,1)} %values_h.1, bf16[32,1024]{1,0:T(8,128)(2,1)} %outw_h.1, s32[4,4,8]{2,1,0:T(4,128)} %ids_h.1, ...), custom_call_target="tpu_custom_call" | custom-call | tf_op jit(solution)/shard_map/decoder_layer/pallas_call | solution.py:319
  37.6 1.4 %copy.13 = bf16[4,4,1024]{2,1,0:T(4,128)(2,1)} copy(bf16[4,4,1024]{2,1,0:T(4,128)(2,1)} %decoder_layer.1) | data formatting | bytes 65536

commit v2 on v1

--- a/solution.py
+++ b/solution.py
@@ -102,7 +102,7 @@
     front = jnp.where(top_rows, lens[0], lens[1])
     rear = jnp.where(top_rows, lens[2], lens[3])
     position = (jnp.where(low_half, front, rear) + jnp.bitwise_and(sub, 3)).astype(F32)
-    angles = position * rates_v[...]
+    angles = position * jnp.broadcast_to(rates_v[...], (8, 128))
     cosine = jnp.cos(angles)
     sine = jnp.sin(angles)
     c_qkv0.wait()
@@ -312,15 +312,13 @@
 
 def per_device(*args):
     half = np.arange(128) % 32
-    rates = np.broadcast_to(
-        (ROPE_BASE ** (-2.0 * half / 64.0)).astype(np.float32)[None, :], (8, 128)
-    )
+    rates = (ROPE_BASE ** (-2.0 * half / 64.0)).astype(np.float32)
     anywhere = pl.BlockSpec(memory_space=pl.ANY)
     return pl.pallas_call(
         kernel,
-        out_shape=jax.ShapeDtypeStruct((4, 4, 1024), BF16),
+        out_shape=pltpu.VMEM((4, 4, 1024), BF16),
         in_specs=[anywhere] * 11,
-        out_specs=anywhere,
+        out_specs=pl.BlockSpec(memory_space=pltpu.VMEM),
         scratch_shapes=[
             pltpu.VMEM((4, 4, 1024), BF16),
             pltpu.SMEM((4,), jnp.int32),
@@ -331,7 +329,7 @@
             pltpu.VMEM((4, 4, 8), jnp.int32),
             pltpu.VMEM((1024, 1024), BF16),
             pltpu.VMEM((512, 1024), BF16),
-            pltpu.VMEM((8, 128), F32),
+            pltpu.VMEM((1, 128), F32),
             pltpu.VMEM((8, 128), BF16),
             pltpu.VMEM((32, 8, 128), BF16),
             pltpu.VMEM((4, 32, 1024), BF16),
@@ -350,7 +348,7 @@
         ],
         compiler_params=pltpu.CompilerParams(collective_id=0, has_side_effects=True),
         name="decoder_layer",
-    )(*args, jnp.asarray(rates))
+    )(*args, jnp.asarray(rates).reshape(1, 128))
 
 
 def solution(mesh):

time: 39.2 us -> 37 us (0.944)
  local copies, waits for them, and re-layouts: 2.63 us -> 0.62 us
    another operation x1 -> x0, local copies, waits for them, and re-layouts: 1.25 us -> none
    unnamed x1, local copies, waits for them, and re-layouts: 1.39 us -> 0.62 us
where the time goes in v2:
time: 37 us; the launch traced here: 36.9 us
  Pallas kernels  36.3 us (98%)
  local copies, waits for them, and re-layouts  0.62 us (2%)
    pallas_call x1, Pallas kernels, per_device(): pl.pallas_call(kernel, out_shape=pltpu.VMEM((4, 4, 1024), BF16), in_specs...  36.3 us

profile of v2, /device:TPU:1, one launch (start us, length us, event | category | flops | bytes accessed | tf_op | source)
XLA Modules:
  0.0 36.9 jit_solution(11706353114035562434)
XLA Ops:
  0.0 36.3 %decoder_layer.1 = bf16[4,4,1024]{2,1,0:T(4,128)(2,1)S(1)} custom-call(bf16[4,4,1024]{2,1,0:T(4,128)(2,1)} %hidden_h.1, s32[4]{0:T(128)} %lengths_h.1, bf16[64,1024]{1,0:T(8,128)(2,1)} %qkv_h.1, bf16[4,128,512]{2,1,0:T(8,128)(2,1)} %keys_h.1, bf16[4,128,512]{2,1,0:T(8,128)(2,1)} %values_h.1, bf16[32,1024]{1,0:T(8,128)(2,1)} %outw_h.1, s32[4,4,8]{2,1,0:T(4,128)} %ids_h.1, ...), custom_call_target="tpu_custom_call" | custom-call | tf_op jit(solution)/shard_map/decoder_layer/pallas_call | solution.py:317
  36.3 0.6 %copy.13 = bf16[4,4,1024]{2,1,0:T(4,128)(2,1)} copy(bf16[4,4,1024]{2,1,0:T(4,128)(2,1)S(1)} %decoder_layer.1) | data formatting | bytes 65536

commit v3 on v2

v3 whole, which is shorter than its diff:
```python
import functools

import jax
import jax.numpy as jnp
import numpy as np
from jax import lax
from jax.experimental import pallas as pl
from jax.experimental.pallas import tpu as pltpu
from jax.sharding import PartitionSpec as P

EPSILON = 1e-05
ROPE_BASE = 10000.0
NEGATIVE = -1e30
MESH = pl.DeviceIdType.MESH
F32 = jnp.float32
BF16 = jnp.bfloat16


def hops(offset):
    return min(offset, 4 - offset)


PEERS = sorted(
    [(dx, dz, dc) for dx in range(4) for dz in range(4) for dc in range(2) if dx or dz or dc],
    key=lambda o: -(hops(o[0]) + hops(o[1]) + 0.5 * o[2]),
)


def stack_rows(pieces):
    return jnp.concatenate(pieces, axis=0)


def kernel(
    hidden_h, lengths_h, qkv_h, keys_h, values_h, outw_h, ids_h, comb_h, gate_h, down_h, rates_h,
    out_h,
    hidden_v, lengths_s, qkv_v, keys_v, values_v, ids_v, comb_v, gate_v, down_v, rates_v,
    qsend, qbuf, wbuf, asend, abuf, pick, rsend, rbuf, kept, ysend, ypair, hsend, hbuf,
    lsem, ssem, rsem,
):
    me = lax.axis_index("tp")
    x = lax.div(me, 8)
    z = lax.rem(lax.div(me, 2), 4)
    c = lax.rem(me, 2)

    def device(offset):
        dx, dz, dc = offset
        px = lax.rem(x + dx, 4) if dx else x
        pz = lax.rem(z + dz, 4) if dz else z
        pc = lax.rem(c + dc, 2) if dc else c
        return px, pz, pc

    def index(offset):
        px, pz, pc = device(offset)
        return px * 8 + pz * 2 + pc

    peers = [index(o) for o in PEERS]

    barrier = pltpu.get_barrier_semaphore()
    for p in peers:
        pl.semaphore_signal(barrier, inc=1, device_id={"tp": p}, device_id_type=MESH)

    def load(src, dst, i):
        copy = pltpu.make_async_copy(src, dst, lsem.at[i])
        copy.start()
        return copy

    c_hidden = load(hidden_h, hidden_v, 0)
    c_len = load(lengths_h, lengths_s, 1)
    c_qkv0 = load(qkv_h, qkv_v.at[pl.ds(0, 64)], 2)
    c_qkv1 = load(qkv_h, qkv_v.at[pl.ds(64, 64)], 3)
    c_rates = load(rates_h, rates_v, 4)
    c_keys = load(keys_h, keys_v, 5)
    c_values = load(values_h, values_v, 6)
    c_ids = load(ids_h, ids_v, 7)
    c_comb = load(comb_h, comb_v, 8)
    c_gate = load(gate_h.at[0], gate_v, 9)
    c_down = load(down_h.at[0], down_v, 10)

    def send(src, dst, phase, p):
        pltpu.make_async_remote_copy(
            src_ref=src, dst_ref=dst, send_sem=ssem.at[phase], recv_sem=rsem.at[phase],
            device_id={"tp": p}, device_id_type=MESH,
        ).start()

    def wait_bytes(ref, sem):
        pltpu.make_async_copy(ref, ref, sem).wait()

    sub = lax.broadcasted_iota(jnp.int32, (8, 128), 0)
    lane = lax.broadcasted_iota(jnp.int32, (8, 128), 1)
    low_half = lane < 64
    top_rows = sub < 4

    c_hidden.wait()
    rows = stack_rows([hidden_v[r].astype(F32) for r in range(4)])
    normed = (
        rows * lax.rsqrt(jnp.mean(rows * rows, axis=-1, keepdims=True) + EPSILON)
    ).astype(BF16)
    c_len.wait()
    lens = [lengths_s[r] for r in range(4)]
    c_rates.wait()
    front = jnp.where(top_rows, lens[0], lens[1])
    rear = jnp.where(top_rows, lens[2], lens[3])
    position = (jnp.where(low_half, front, rear) + jnp.bitwise_and(sub, 3)).astype(F32)
    angles = position * jnp.broadcast_to(rates_v[...], (8, 128))
    cosine = jnp.cos(angles)
    sine = jnp.sin(angles)
    c_qkv0.wait()
    c_qkv1.wait()
    head = lax.dot_general(
        normed, qkv_v[...], (((1,), (1,)), ((), ())), preferred_element_type=F32
    )
    head = head.astype(BF16).astype(F32)
    packed = jnp.where(low_half, head[0:8], head[8:16])
    ahead = pltpu.roll(packed, 96, 1)
    behind = pltpu.roll(packed, 32, 1)
    first = jnp.bitwise_and(lane, 63) < 32
    turned = packed * cosine + jnp.where(first, -ahead, behind) * sine
    turned = turned.astype(BF16).astype(F32)
    query = turned * 0.125
    place = jnp.broadcast_to(lax.rem(me, 4), (8, 128))
    query = jnp.where(place >= 2, pltpu.roll(query, 64, 1), query)
    query = jnp.where(jnp.bitwise_and(place, 1) == 1, pltpu.roll(query, 2, 0), query)
    query = jnp.where(place >= 2, pltpu.roll(query, 4, 0), query)
    whole_me = jnp.broadcast_to(me, (8, 128))
    qsend[...] = jnp.where(
        whole_me < 16, query, jnp.where(whole_me < 24, turned, packed)
    ).astype(BF16)
    for k in range(8):
        kept[k // 4, :, (k % 4) * 128 : (k % 4) * 128 + 128] = rows[:, k * 128 : k * 128 + 128]
    target = lax.broadcasted_iota(jnp.int32, (128, 512), 0)
    source = lax.broadcasted_iota(jnp.int32, (128, 512), 1)
    token = 2 * jnp.bitwise_and(lax.shift_right_logical(source, 4), 7) + jnp.bitwise_and(source, 1)
    column = jnp.bitwise_and(lax.shift_right_logical(source, 1), 7)
    pick[...] = jnp.where(target == column * 16 + token, 1.0, 0.0).astype(BF16)

    pl.semaphore_wait(barrier, 31)
    for p in peers:
        send(qsend, qbuf.at[me], 0, p)
    pltpu.make_async_copy(qsend, qbuf.at[me], rsem.at[0]).start()

    for dz in (2, 1, 3):
        send(outw_h, wbuf.at[2 * z + c], 1, x * 8 + lax.rem(z + dz, 4) * 2 + c)
    pltpu.make_async_copy(outw_h, wbuf.at[2 * z + c], rsem.at[1]).start()

    wait_bytes(qbuf, rsem.at[0])
    heads = [qbuf[h].astype(F32) for h in range(16)]
    pair = lax.shift_right_logical(sub, 1)
    mixed = []
    for q in range(4):
        row = []
        for n in range(4):
            tile = heads[4 * n + (3 - q) % 4]
            for p in range(3):
                tile = jnp.where(pair == p, heads[4 * n + (p - q) % 4], tile)
            row.append(tile)
        mixed.append(row)
    rear_head = [jnp.bitwise_and(pair - q, 3) >= 2 for q in range(4)]
    fits = [rear_head[q] != low_half for q in range(4)]
    c_keys.wait()
    c_values.wait()
    zero = jnp.zeros((8, 128), F32)
    cell = lax.broadcasted_iota(jnp.int32, (64, 128), 1) + me * 128
    for r in range(4):
        tiles = []
        for sp in range(2):
            q = 2 * (r % 2) + sp
            row = []
            for n in range(4):
                tile = mixed[q][n] if r < 2 else pltpu.roll(mixed[q][n], 64, 1)
                row.append(jnp.where(fits[q], tile, 0.0))
            tiles.append(row)
        columns = [
            jnp.concatenate(
                [tiles[sp][n] if n == k else zero for n in range(4) for sp in range(2)], axis=0
            )
            for k in range(4)
        ]
        queries = jnp.concatenate(columns, axis=1).astype(BF16)
        scores = lax.dot_general(
            queries, keys_v[r], (((1,), (1,)), ((), ())), preferred_element_type=F32
        )
        live = cell < lens[r]
        masked = jnp.where(live, scores, NEGATIVE)
        peak = jnp.max(masked, axis=-1, keepdims=True)
        weights = jnp.where(live, jnp.exp(masked - peak), 0.0)
        total = jnp.sum(weights, axis=-1, keepdims=True)
        sums = jnp.dot(weights.astype(BF16), values_v[r], preferred_element_type=F32)
        for n in range(4):
            for sp in range(2):
                b = 8 * (2 * n + sp)
                o = sums[b : b + 8, n * 128 : n * 128 + 128]
                o = jnp.where(rear_head[2 * (r % 2) + sp], pltpu.roll(o, 64, 1), o)
                stats = jnp.where(
                    lane < 96,
                    jnp.broadcast_to(peak[b : b + 8], (8, 128)),
                    jnp.broadcast_to(total[b : b + 8], (8, 128)),
                )
                asend[n * 8 + r * 2 + sp] = jnp.where(low_half, o, stats)

    for p in peers:
        send(asend.at[p], abuf.at[me], 2, p)
    pltpu.make_async_copy(asend.at[me], abuf.at[me], rsem.at[2]).start()

    partner = me + 1 - 2 * c
    wait_bytes(wbuf.at[pl.ds(0, 4)], rsem.at[1])
    for k in range(4):
        send(wbuf.at[2 * k + c], wbuf.at[2 * k + c], 3, partner)

    late = jnp.broadcast_to(lax.rem(z, 2), (8, 128)) == 1
    rear_half = jnp.broadcast_to(lax.div(z, 2), (8, 128)) == 1
    q_own = 2 * lax.rem(z, 2) + c
    tile = qbuf[4 * x + lax.rem(7 - q_own, 4)].astype(F32)
    for p in range(3):
        tile = jnp.where(pair == p, qbuf[4 * x + lax.rem(p + 4 - q_own, 4)].astype(F32), tile)
    head_place = jnp.bitwise_and(pair - jnp.broadcast_to(q_own, (8, 128)), 3)
    own_rear = head_place >= 2
    own_queries = jnp.where(
        low_half, jnp.where(own_rear != rear_half, pltpu.roll(tile, 64, 1), tile), 0.0
    )

    def own_rows(i):
        v = qbuf[i].astype(F32)
        v = jnp.where(rear_half, pltpu.roll(v, 64, 1), v)
        return jnp.where(late, pltpu.roll(v, 4, 0), v)

    def per_head(front, rear):
        return [
            jnp.where(
                own_rear,
                jnp.broadcast_to(rear[s : s + 1], (8, 128)),
                jnp.broadcast_to(front[s : s + 1], (8, 128)),
            )
            for s in range(4)
        ]

    new_keys = per_head(own_rows(16 + 2 * x), own_rows(17 + 2 * x))
    new_values = per_head(own_rows(24 + 2 * x), own_rows(25 + 2 * x))
    step = 2 * jnp.broadcast_to(c, (8, 128)) + jnp.bitwise_and(sub, 1)
    new_scores = []
    for s in range(4):
        score = jnp.sum(
            own_queries * new_keys[s], axis=-1, keepdims=True
        )
        new_scores.append(
            jnp.where(step >= s, jnp.broadcast_to(score, (8, 128)), NEGATIVE)
        )
    new_peak = functools.reduce(jnp.maximum, new_scores)
    new_weights = [jnp.exp(v - new_peak) for v in new_scores]
    new_total = functools.reduce(jnp.add, new_weights)
    new_sum = functools.reduce(
        jnp.add,
        [
            new_weights[s].astype(BF16).astype(F32) * new_values[s]
            for s in range(4)
        ],
    )
    c_ids.wait()
    c_comb.wait()
    factors = [
        jnp.sum(
            jnp.where(ids_v[r] == me, comb_v[r], 0).astype(F32), axis=-1, keepdims=True
        )
        * (1.0 / 65536.0)
        for r in range(4)
    ]
    factor = stack_rows(factors)
    wait_bytes(wbuf.at[pl.ds(0, 4)], rsem.at[3])

    wait_bytes(abuf, rsem.at[2])
    peaks = [jnp.broadcast_to(abuf[b][:, 64:65], (8, 128)) for b in range(32)]
    top = functools.reduce(jnp.maximum, peaks + [new_peak])
    total_all = jnp.zeros((8, 128), F32)
    for b in range(32):
        total_all = total_all + jnp.exp(peaks[b] - top) * abuf[b]
    carried = jnp.exp(new_peak - top)
    denominator = jnp.broadcast_to(total_all[:, 96:97], (8, 128)) + carried * new_total
    attended = jnp.where(low_half, (total_all + carried * new_sum) / denominator, 0.0)
    attended = attended + pltpu.roll(attended, 64, 1)
    half = lax.shift_right_logical(lane, 6)
    attended = jnp.concatenate(
        [
            jnp.where(half == head_place, attended, 0.0),
            jnp.where(half + 2 == head_place, attended, 0.0),
        ],
        axis=1,
    ).astype(BF16)
    product = jnp.dot(
        attended, wbuf[...].reshape(256, 1024), preferred_element_type=F32
    )
    product = product + pltpu.roll(product, 4, 0)
    product = product + pltpu.roll(product, 2, 0)
    parts = []
    for m in range(2):
        part = product[:, m * 512 + 384 : m * 512 + 512]
        for k in range(3):
            at = m * 512 + k * 128
            part = jnp.where(pair == k, product[:, at : at + 128], part)
        parts.append(part)
    rsend[...] = jnp.concatenate(parts, axis=0).astype(BF16)
    for p in peers:
        send(rsend, rbuf.at[me], 4, p)
    pltpu.make_async_copy(rsend, rbuf.at[me], rsem.at[4]).start()
    c_gate.wait()
    c_down.wait()
    wait_bytes(rbuf, rsem.at[4])
    projected = jnp.dot(
        pick[...], rbuf[...].reshape(512, 128), preferred_element_type=F32
    )
    rows = []
    for k in range(8):
        at = pl.ds((k % 4) * 128, 128)
        row = kept[k // 4, :, at] + projected[16 * k : 16 * k + 16]
        kept[k // 4, :, at] = row
        rows.append(row)
    rows = jnp.concatenate(rows, axis=1)
    normed = (
        rows * lax.rsqrt(jnp.mean(rows * rows, axis=-1, keepdims=True) + EPSILON)
    ).astype(BF16)
    united = jnp.dot(normed, gate_v[...], preferred_element_type=F32)
    gate = united[:, :512]
    activation = (gate / (1.0 + jnp.exp(-gate)) * united[:, 512:]).astype(BF16)

    def half_outcome(half):
        start = pl.multiple_of(half * 512, 512)
        return factor * jnp.dot(
            activation, down_v[:, pl.ds(start, 512)], preferred_element_type=F32
        )

    ysend[...] = half_outcome(1 - c).astype(BF16)
    send(ysend, ypair, 5, partner)
    mine = half_outcome(c)
    wait_bytes(ypair, rsem.at[5])
    hsend[...] = (mine + ypair[...].astype(F32)).astype(BF16)
    chip = 4 * x + z
    for o in PEERS:
        if o[2] == 0:
            send(hsend, hbuf.at[chip], 6, index(o))
    pltpu.make_async_copy(hsend, hbuf.at[chip], rsem.at[6]).start()
    wait_bytes(hbuf, rsem.at[6])
    final = kept[c]
    for k in range(16):
        final = final + hbuf[k].astype(F32)
    own_half = pl.ds(pl.multiple_of(c * 512, 512), 512)
    for r in range(4):
        out_h[r, :, own_half] = final[4 * r : 4 * r + 4].astype(BF16)
    send(out_h.at[:, :, own_half], out_h.at[:, :, own_half], 7, partner)
    wait_bytes(out_h.at[:, :, pl.ds(pl.multiple_of(512 - c * 512, 512), 512)], rsem.at[7])

    wait_bytes(qbuf.at[pl.ds(0, 31)], ssem.at[0])
    wait_bytes(wbuf.at[pl.ds(0, 3)], ssem.at[1])
    wait_bytes(abuf.at[pl.ds(0, 31)], ssem.at[2])
    wait_bytes(wbuf.at[pl.ds(0, 4)], ssem.at[3])
    wait_bytes(rbuf.at[pl.ds(0, 31)], ssem.at[4])
    wait_bytes(ypair, ssem.at[5])
    wait_bytes(hbuf.at[pl.ds(0, 15)], ssem.at[6])
    wait_bytes(out_h.at[:, :, own_half], ssem.at[7])


def per_device(*args):
    half = np.arange(128) % 32
    rates = (ROPE_BASE ** (-2.0 * half / 64.0)).astype(np.float32)
    anywhere = pl.BlockSpec(memory_space=pl.ANY)
    return pl.pallas_call(
        kernel,
        out_shape=pltpu.VMEM((4, 4, 1024), BF16),
        in_specs=[anywhere] * 11,
        out_specs=pl.BlockSpec(memory_space=pltpu.VMEM),
        scratch_shapes=[
            pltpu.VMEM((4, 4, 1024), BF16),
            pltpu.SMEM((4,), jnp.int32),
            pltpu.VMEM((128, 1024), BF16),
            pltpu.VMEM((4, 128, 512), BF16),
            pltpu.VMEM((4, 128, 512), BF16),
            pltpu.VMEM((4, 4, 8), jnp.int32),
            pltpu.VMEM((4, 4, 8), jnp.int32),
            pltpu.VMEM((1024, 1024), BF16),
            pltpu.VMEM((512, 1024), BF16),
            pltpu.VMEM((1, 128), F32),
            pltpu.VMEM((8, 128), BF16),
            pltpu.VMEM((32, 8, 128), BF16),
            pltpu.VMEM((8, 32, 1024), BF16),
            pltpu.VMEM((32, 8, 128), F32),
            pltpu.VMEM((32, 8, 128), F32),
            pltpu.VMEM((128, 512), BF16),
            pltpu.VMEM((16, 128), BF16),
            pltpu.VMEM((32, 16, 128), BF16),
            pltpu.VMEM((2, 16, 512), F32),
            pltpu.VMEM((16, 512), BF16),
            pltpu.VMEM((16, 512), BF16),
            pltpu.VMEM((16, 512), BF16),
            pltpu.VMEM((16, 16, 512), BF16),
            pltpu.SemaphoreType.DMA((11,)),
            pltpu.SemaphoreType.DMA((8,)),
            pltpu.SemaphoreType.DMA((8,)),
        ],
        compiler_params=pltpu.CompilerParams(collective_id=0, has_side_effects=True),
        name="decoder_layer",
    )(*args, jnp.asarray(rates).reshape(1, 128))


def solution(mesh):
    in_specs = (
        P("req", None, None),
        P("req"),
        P("tp", None),
        P("req", "tp", None),
        P("req", "tp", None),
        P("tp", None),
        P("req", None, None),
        P("req", None, None),
        P("tp", None, None),
        P("tp", None, None),
    )
    out_specs = P("req", None, None)
    return jax.shard_map(
        per_device, mesh=mesh, in_specs=in_specs, out_specs=out_specs, check_vma=False
    )
```

time: 37 us -> 33.3 us (0.90)
  Pallas kernels: 36.3 us -> 32.5 us
    pallas_call x1, Pallas kernels: 36.3 us -> 32.5 us  [per_device(): pl.pallas_call(kernel, out_shape=pltpu.VMEM((4, 4, 1024), BF16), in_specs...]
where the time goes in v3:
time: 33.3 us; the launch traced here: 33.2 us
  Pallas kernels  32.5 us (98%)
  local copies, waits for them, and re-layouts  0.62 us (2%)
    pallas_call x1, Pallas kernels, per_device(): pl.pallas_call(kernel, out_shape=pltpu.VMEM((4, 4, 1024), BF16), in_specs...  32.5 us

profile of v3, /device:TPU:1, one launch (start us, length us, event | category | flops | bytes accessed | tf_op | source)
XLA Modules:
  0.0 33.2 jit_solution(8101496426933189566)
XLA Ops:
  0.0 32.5 %decoder_layer.1 = bf16[4,4,1024]{2,1,0:T(4,128)(2,1)S(1)} custom-call(bf16[4,4,1024]{2,1,0:T(4,128)(2,1)} %hidden_h.1, s32[4]{0:T(128)} %lengths_h.1, bf16[64,1024]{1,0:T(8,128)(2,1)} %qkv_h.1, bf16[4,128,512]{2,1,0:T(8,128)(2,1)} %keys_h.1, bf16[4,128,512]{2,1,0:T(8,128)(2,1)} %values_h.1, bf16[32,1024]{1,0:T(8,128)(2,1)} %outw_h.1, s32[4,4,8]{2,1,0:T(4,128)} %ids_h.1, ...), custom_call_target="tpu_custom_call" | custom-call | tf_op jit(solution)/shard_map/decoder_layer/pallas_call | solution.py:363
  32.5 0.6 %copy.13 = bf16[4,4,1024]{2,1,0:T(4,128)(2,1)} copy(bf16[4,4,1024]{2,1,0:T(4,128)(2,1)S(1)} %decoder_layer.1) | data formatting | bytes 65536

commit v4 on v3

--- a/solution.py
+++ b/solution.py
@@ -34,7 +34,7 @@
     hidden_h, lengths_h, qkv_h, keys_h, values_h, outw_h, ids_h, comb_h, gate_h, down_h, rates_h,
     out_h,
     hidden_v, lengths_s, qkv_v, keys_v, values_v, ids_v, comb_v, gate_v, down_v, rates_v,
-    qsend, qbuf, wbuf, asend, abuf, pick, rsend, rbuf, kept, ysend, ypair, hsend, hbuf,
+    qsend, qbuf, wbuf, asend, abuf, pick, rsend, rbuf, kept, hsend, hbuf,
     lsem, ssem, rsem,
 ):
     me = lax.axis_index("tp")
@@ -54,6 +54,8 @@
         return px * 8 + pz * 2 + pc
 
     peers = [index(o) for o in PEERS]
+
+    partner = me + 1 - 2 * c
 
     barrier = pltpu.get_barrier_semaphore()
     for p in peers:
@@ -73,8 +75,10 @@
     c_values = load(values_h, values_v, 6)
     c_ids = load(ids_h, ids_v, 7)
     c_comb = load(comb_h, comb_v, 8)
-    c_gate = load(gate_h.at[0], gate_v, 9)
-    c_down = load(down_h.at[0], down_v, 10)
+    c_gate = load(gate_h.at[0], gate_v.at[c], 9)
+    own_half = pl.ds(pl.multiple_of(c * 512, 512), 512)
+    other_half = pl.ds(pl.multiple_of(512 - c * 512, 512), 512)
+    c_down = load(down_h.at[0, :, own_half], down_v.at[c], 10)
 
     def send(src, dst, phase, p):
         pltpu.make_async_remote_copy(
@@ -159,7 +163,7 @@
     c_keys.wait()
     c_values.wait()
     zero = jnp.zeros((8, 128), F32)
-    cell = lax.broadcasted_iota(jnp.int32, (64, 128), 1) + me * 128
+    all_scores = []
     for r in range(4):
         tiles = []
         for sp in range(2):
@@ -176,35 +180,42 @@
             for k in range(4)
         ]
         queries = jnp.concatenate(columns, axis=1).astype(BF16)
-        scores = lax.dot_general(
-            queries, keys_v[r], (((1,), (1,)), ((), ())), preferred_element_type=F32
-        )
-        live = cell < lens[r]
-        masked = jnp.where(live, scores, NEGATIVE)
-        peak = jnp.max(masked, axis=-1, keepdims=True)
-        weights = jnp.where(live, jnp.exp(masked - peak), 0.0)
-        total = jnp.sum(weights, axis=-1, keepdims=True)
-        sums = jnp.dot(weights.astype(BF16), values_v[r], preferred_element_type=F32)
+        all_scores.append(
+            lax.dot_general(
+                queries, keys_v[r], (((1,), (1,)), ((), ())), preferred_element_type=F32
+            )
+        )
+    cell = lax.broadcasted_iota(jnp.int32, (64, 128), 1) + me * 128
+    live = [cell < lens[r] for r in range(4)]
+    masked = [jnp.where(live[r], all_scores[r], NEGATIVE) for r in range(4)]
+    peaks = [jnp.max(masked[r], axis=-1, keepdims=True) for r in range(4)]
+    weights = [jnp.where(live[r], jnp.exp(masked[r] - peaks[r]), 0.0) for r in range(4)]
+    sums = [
+        jnp.dot(weights[r].astype(BF16), values_v[r], preferred_element_type=F32)
+        for r in range(4)
+    ]
+    totals = [jnp.sum(weights[r], axis=-1, keepdims=True) for r in range(4)]
+    for r in range(4):
+        stats = jnp.where(
+            lax.broadcasted_iota(jnp.int32, (64, 128), 1) < 96, peaks[r], totals[r]
+        )
         for n in range(4):
             for sp in range(2):
                 b = 8 * (2 * n + sp)
-                o = sums[b : b + 8, n * 128 : n * 128 + 128]
+                o = sums[r][b : b + 8, n * 128 : n * 128 + 128]
                 o = jnp.where(rear_head[2 * (r % 2) + sp], pltpu.roll(o, 64, 1), o)
-                stats = jnp.where(
-                    lane < 96,
-                    jnp.broadcast_to(peak[b : b + 8], (8, 128)),
-                    jnp.broadcast_to(total[b : b + 8], (8, 128)),
-                )
-                asend[n * 8 + r * 2 + sp] = jnp.where(low_half, o, stats)
+                asend[n * 8 + r * 2 + sp] = jnp.where(low_half, o, stats[b : b + 8])
 
     for p in peers:
         send(asend.at[p], abuf.at[me], 2, p)
     pltpu.make_async_copy(asend.at[me], abuf.at[me], rsem.at[2]).start()
 
-    partner = me + 1 - 2 * c
     wait_bytes(wbuf.at[pl.ds(0, 4)], rsem.at[1])
     for k in range(4):
         send(wbuf.at[2 * k + c], wbuf.at[2 * k + c], 3, partner)
+
+    send(gate_h.at[0], gate_v.at[c], 5, partner)
+    send(down_h.at[0, :, other_half], down_v.at[c], 8, partner)
 
     late = jnp.broadcast_to(lax.rem(z, 2), (8, 128)) == 1
     rear_half = jnp.broadcast_to(lax.div(z, 2), (8, 128)) == 1
@@ -257,13 +268,19 @@
     c_ids.wait()
     c_comb.wait()
     factors = [
-        jnp.sum(
-            jnp.where(ids_v[r] == me, comb_v[r], 0).astype(F32), axis=-1, keepdims=True
+        stack_rows(
+            [
+                jnp.sum(
+                    jnp.where(ids_v[r] == me - c + e, comb_v[r], 0).astype(F32),
+                    axis=-1,
+                    keepdims=True,
+                )
+                for r in range(4)
+            ]
         )
         * (1.0 / 65536.0)
-        for r in range(4)
+        for e in range(2)
     ]
-    factor = stack_rows(factors)
     wait_bytes(wbuf.at[pl.ds(0, 4)], rsem.at[3])
 
     wait_bytes(abuf, rsem.at[2])
@@ -316,21 +333,20 @@
     normed = (
         rows * lax.rsqrt(jnp.mean(rows * rows, axis=-1, keepdims=True) + EPSILON)
     ).astype(BF16)
-    united = jnp.dot(normed, gate_v[...], preferred_element_type=F32)
-    gate = united[:, :512]
-    activation = (gate / (1.0 + jnp.exp(-gate)) * united[:, 512:]).astype(BF16)
-
-    def half_outcome(half):
-        start = pl.multiple_of(half * 512, 512)
-        return factor * jnp.dot(
-            activation, down_v[:, pl.ds(start, 512)], preferred_element_type=F32
-        )
-
-    ysend[...] = half_outcome(1 - c).astype(BF16)
-    send(ysend, ypair, 5, partner)
-    mine = half_outcome(c)
-    wait_bytes(ypair, rsem.at[5])
-    hsend[...] = (mine + ypair[...].astype(F32)).astype(BF16)
+    wait_bytes(gate_v.at[0], rsem.at[5])
+    wait_bytes(down_v.at[0], rsem.at[8])
+    activations = []
+    for e in range(2):
+        united = jnp.dot(normed, gate_v[e], preferred_element_type=F32)
+        gate = united[:, :512]
+        activations.append(
+            (gate / (1.0 + jnp.exp(-gate)) * united[:, 512:] * factors[e]).astype(BF16)
+        )
+    hsend[...] = jnp.dot(
+        jnp.concatenate(activations, axis=1),
+        down_v[...].reshape(1024, 512),
+        preferred_element_type=F32,
+    ).astype(BF16)
     chip = 4 * x + z
     for o in PEERS:
         if o[2] == 0:
@@ -340,18 +356,18 @@
     final = kept[c]
     for k in range(16):
         final = final + hbuf[k].astype(F32)
-    own_half = pl.ds(pl.multiple_of(c * 512, 512), 512)
     for r in range(4):
         out_h[r, :, own_half] = final[4 * r : 4 * r + 4].astype(BF16)
     send(out_h.at[:, :, own_half], out_h.at[:, :, own_half], 7, partner)
-    wait_bytes(out_h.at[:, :, pl.ds(pl.multiple_of(512 - c * 512, 512), 512)], rsem.at[7])
+    wait_bytes(out_h.at[:, :, other_half], rsem.at[7])
 
     wait_bytes(qbuf.at[pl.ds(0, 31)], ssem.at[0])
     wait_bytes(wbuf.at[pl.ds(0, 3)], ssem.at[1])
     wait_bytes(abuf.at[pl.ds(0, 31)], ssem.at[2])
     wait_bytes(wbuf.at[pl.ds(0, 4)], ssem.at[3])
     wait_bytes(rbuf.at[pl.ds(0, 31)], ssem.at[4])
-    wait_bytes(ypair, ssem.at[5])
+    wait_bytes(gate_v.at[0], ssem.at[5])
+    wait_bytes(down_v.at[0], ssem.at[8])
     wait_bytes(hbuf.at[pl.ds(0, 15)], ssem.at[6])
     wait_bytes(out_h.at[:, :, own_half], ssem.at[7])
 
@@ -373,8 +389,8 @@
             pltpu.VMEM((4, 128, 512), BF16),
             pltpu.VMEM((4, 4, 8), jnp.int32),
             pltpu.VMEM((4, 4, 8), jnp.int32),
-            pltpu.VMEM((1024, 1024), BF16),
-            pltpu.VMEM((512, 1024), BF16),
+            pltpu.VMEM((2, 1024, 1024), BF16),
+            pltpu.VMEM((2, 512, 512), BF16),
             pltpu.VMEM((1, 128), F32),
             pltpu.VMEM((8, 128), BF16),
             pltpu.VMEM((32, 8, 128), BF16),
@@ -386,12 +402,10 @@
             pltpu.VMEM((32, 16, 128), BF16),
             pltpu.VMEM((2, 16, 512), F32),
             pltpu.VMEM((16, 512), BF16),
-            pltpu.VMEM((16, 512), BF16),
-            pltpu.VMEM((16, 512), BF16),
             pltpu.VMEM((16, 16, 512), BF16),
             pltpu.SemaphoreType.DMA((11,)),
-            pltpu.SemaphoreType.DMA((8,)),
-            pltpu.SemaphoreType.DMA((8,)),
+            pltpu.SemaphoreType.DMA((9,)),
+            pltpu.SemaphoreType.DMA((9,)),
         ],
         compiler_params=pltpu.CompilerParams(collective_id=0, has_side_effects=True),
         name="decoder_layer",

time: 33.3 us -> 31.7 us (0.952)
  Pallas kernels: 32.5 us -> 31 us
    pallas_call x1, Pallas kernels: 32.5 us -> 31 us  [per_device(): pl.pallas_call(kernel, out_shape=pltpu.VMEM((4, 4, 1024), BF16), in_specs...]
where the time goes in v4:
time: 31.7 us; the launch traced here: 31.6 us
  Pallas kernels  31 us (98%)
  local copies, waits for them, and re-layouts  0.62 us (2%)
    pallas_call x1, Pallas kernels, per_device(): pl.pallas_call(kernel, out_shape=pltpu.VMEM((4, 4, 1024), BF16), in_specs...  31 us

profile of v4, /device:TPU:1, one launch (start us, length us, event | category | flops | bytes accessed | tf_op | source)
XLA Modules:
  0.0 31.6 jit_solution(4224670071953510415)
XLA Ops:
  0.0 31.0 %decoder_layer.1 = bf16[4,4,1024]{2,1,0:T(4,128)(2,1)S(1)} custom-call(bf16[4,4,1024]{2,1,0:T(4,128)(2,1)} %hidden_h.1, s32[4]{0:T(128)} %lengths_h.1, bf16[64,1024]{1,0:T(8,128)(2,1)} %qkv_h.1, bf16[4,128,512]{2,1,0:T(8,128)(2,1)} %keys_h.1, bf16[4,128,512]{2,1,0:T(8,128)(2,1)} %values_h.1, bf16[32,1024]{1,0:T(8,128)(2,1)} %outw_h.1, s32[4,4,8]{2,1,0:T(4,128)} %ids_h.1, ...), custom_call_target="tpu_custom_call" | custom-call | tf_op jit(solution)/shard_map/decoder_layer/pallas_call | solution.py:379
  31.0 0.6 %copy.13 = bf16[4,4,1024]{2,1,0:T(4,128)(2,1)} copy(bf16[4,4,1024]{2,1,0:T(4,128)(2,1)S(1)} %decoder_layer.1) | data formatting | bytes 65536

commit v5 on v4

--- a/solution.py
+++ b/solution.py
@@ -24,6 +24,15 @@
     [(dx, dz, dc) for dx in range(4) for dz in range(4) for dc in range(2) if dx or dz or dc],
     key=lambda o: -(hops(o[0]) + hops(o[1]) + 0.5 * o[2]),
 )
+
+
+def tree(op, items):
+    while len(items) > 1:
+        items = [
+            op(items[k], items[k + 1]) if k + 1 < len(items) else items[k]
+            for k in range(0, len(items), 2)
+        ]
+    return items[0]
 
 
 def stack_rows(pieces):
@@ -78,7 +87,7 @@
     c_gate = load(gate_h.at[0], gate_v.at[c], 9)
     own_half = pl.ds(pl.multiple_of(c * 512, 512), 512)
     other_half = pl.ds(pl.multiple_of(512 - c * 512, 512), 512)
-    c_down = load(down_h.at[0, :, own_half], down_v.at[c], 10)
+    c_down = load(down_h.at[0, :, other_half], down_v.at[c], 10)
 
     def send(src, dst, phase, p):
         pltpu.make_async_remote_copy(
@@ -215,7 +224,7 @@
         send(wbuf.at[2 * k + c], wbuf.at[2 * k + c], 3, partner)
 
     send(gate_h.at[0], gate_v.at[c], 5, partner)
-    send(down_h.at[0, :, other_half], down_v.at[c], 8, partner)
+    send(down_h.at[0, :, own_half], down_v.at[c], 8, partner)
 
     late = jnp.broadcast_to(lax.rem(z, 2), (8, 128)) == 1
     rear_half = jnp.broadcast_to(lax.div(z, 2), (8, 128)) == 1
@@ -285,10 +294,8 @@
 
     wait_bytes(abuf, rsem.at[2])
     peaks = [jnp.broadcast_to(abuf[b][:, 64:65], (8, 128)) for b in range(32)]
-    top = functools.reduce(jnp.maximum, peaks + [new_peak])
-    total_all = jnp.zeros((8, 128), F32)
-    for b in range(32):
-        total_all = total_all + jnp.exp(peaks[b] - top) * abuf[b]
+    top = tree(jnp.maximum, peaks + [new_peak])
+    total_all = tree(jnp.add, [jnp.exp(peaks[b] - top) * abuf[b] for b in range(32)])
     carried = jnp.exp(new_peak - top)
     denominator = jnp.broadcast_to(total_all[:, 96:97], (8, 128)) + carried * new_total
     attended = jnp.where(low_half, (total_all + carried * new_sum) / denominator, 0.0)
@@ -349,13 +356,10 @@
     ).astype(BF16)
     chip = 4 * x + z
     for o in PEERS:
-        if o[2] == 0:
+        if o[2] == 1:
             send(hsend, hbuf.at[chip], 6, index(o))
-    pltpu.make_async_copy(hsend, hbuf.at[chip], rsem.at[6]).start()
     wait_bytes(hbuf, rsem.at[6])
-    final = kept[c]
-    for k in range(16):
-        final = final + hbuf[k].astype(F32)
+    final = kept[c] + tree(jnp.add, [hbuf[k].astype(F32) for k in range(16)])
     for r in range(4):
         out_h[r, :, own_half] = final[4 * r : 4 * r + 4].astype(BF16)
     send(out_h.at[:, :, own_half], out_h.at[:, :, own_half], 7, partner)
@@ -368,7 +372,7 @@
     wait_bytes(rbuf.at[pl.ds(0, 31)], ssem.at[4])
     wait_bytes(gate_v.at[0], ssem.at[5])
     wait_bytes(down_v.at[0], ssem.at[8])
-    wait_bytes(hbuf.at[pl.ds(0, 15)], ssem.at[6])
+    wait_bytes(hbuf, ssem.at[6])
     wait_bytes(out_h.at[:, :, own_half], ssem.at[7])
 
 

time: 31.7 us -> 31.2 us (0.984)
  Pallas kernels: 31 us -> 30.5 us
    pallas_call x1, Pallas kernels: 31 us -> 30.5 us  [per_device(): pl.pallas_call(kernel, out_shape=pltpu.VMEM((4, 4, 1024), BF16), in_specs...]
where the time goes in v5:
time: 31.2 us; the launch traced here: 31.1 us
  Pallas kernels  30.5 us (98%)
  local copies, waits for them, and re-layouts  0.62 us (2%)
    pallas_call x1, Pallas kernels, per_device(): pl.pallas_call(kernel, out_shape=pltpu.VMEM((4, 4, 1024), BF16), in_specs...  30.5 us

profile of v5, /device:TPU:1, one launch (start us, length us, event | category | flops | bytes accessed | tf_op | source)
XLA Modules:
  0.0 31.1 jit_solution(5882977084734714691)
XLA Ops:
  0.0 30.5 %decoder_layer.1 = bf16[4,4,1024]{2,1,0:T(4,128)(2,1)S(1)} custom-call(bf16[4,4,1024]{2,1,0:T(4,128)(2,1)} %hidden_h.1, s32[4]{0:T(128)} %lengths_h.1, bf16[64,1024]{1,0:T(8,128)(2,1)} %qkv_h.1, bf16[4,128,512]{2,1,0:T(8,128)(2,1)} %keys_h.1, bf16[4,128,512]{2,1,0:T(8,128)(2,1)} %values_h.1, bf16[32,1024]{1,0:T(8,128)(2,1)} %outw_h.1, s32[4,4,8]{2,1,0:T(4,128)} %ids_h.1, ...), custom_call_target="tpu_custom_call" | custom-call | tf_op jit(solution)/shard_map/decoder_layer/pallas_call | solution.py:383
  30.5 0.6 %copy.13 = bf16[4,4,1024]{2,1,0:T(4,128)(2,1)} copy(bf16[4,4,1024]{2,1,0:T(4,128)(2,1)S(1)} %decoder_layer.1) | data formatting | bytes 65536

commit v6 on v5

--- a/solution.py
+++ b/solution.py
@@ -67,8 +67,11 @@
     partner = me + 1 - 2 * c
 
     barrier = pltpu.get_barrier_semaphore()
-    for p in peers:
-        pl.semaphore_signal(barrier, inc=1, device_id={"tp": p}, device_id_type=MESH)
+    def greet(some):
+        for p in some:
+            pl.semaphore_signal(barrier, inc=1, device_id={"tp": p}, device_id_type=MESH)
+
+    greet(peers[:10])
 
     def load(src, dst, i):
         copy = pltpu.make_async_copy(src, dst, lsem.at[i])
@@ -80,6 +83,7 @@
     c_qkv0 = load(qkv_h, qkv_v.at[pl.ds(0, 64)], 2)
     c_qkv1 = load(qkv_h, qkv_v.at[pl.ds(64, 64)], 3)
     c_rates = load(rates_h, rates_v, 4)
+    greet(peers[10:])
     c_keys = load(keys_h, keys_v, 5)
     c_values = load(values_h, values_v, 6)
     c_ids = load(ids_h, ids_v, 7)
@@ -103,11 +107,6 @@
     low_half = lane < 64
     top_rows = sub < 4
 
-    c_hidden.wait()
-    rows = stack_rows([hidden_v[r].astype(F32) for r in range(4)])
-    normed = (
-        rows * lax.rsqrt(jnp.mean(rows * rows, axis=-1, keepdims=True) + EPSILON)
-    ).astype(BF16)
     c_len.wait()
     lens = [lengths_s[r] for r in range(4)]
     c_rates.wait()
@@ -117,6 +116,11 @@
     angles = position * jnp.broadcast_to(rates_v[...], (8, 128))
     cosine = jnp.cos(angles)
     sine = jnp.sin(angles)
+    c_hidden.wait()
+    rows = stack_rows([hidden_v[r].astype(F32) for r in range(4)])
+    normed = (
+        rows * lax.rsqrt(jnp.mean(rows * rows, axis=-1, keepdims=True) + EPSILON)
+    ).astype(BF16)
     c_qkv0.wait()
     c_qkv1.wait()
     head = lax.dot_general(

time: 31.2 us -> 31.2 us (level)
  no operation moved by 1% of the time
where the time goes in v6:
time: 31.2 us; the launch traced here: 31.1 us
  Pallas kernels  30.5 us (98%)
  local copies, waits for them, and re-layouts  0.62 us (2%)
    pallas_call x1, Pallas kernels, per_device(): pl.pallas_call(kernel, out_shape=pltpu.VMEM((4, 4, 1024), BF16), in_specs...  30.5 us

profile of v6, /device:TPU:1, one launch (start us, length us, event | category | flops | bytes accessed | tf_op | source)
XLA Modules:
  0.0 31.1 jit_solution(11232500466454377715)
XLA Ops:
  0.0 30.5 %decoder_layer.1 = bf16[4,4,1024]{2,1,0:T(4,128)(2,1)S(1)} custom-call(bf16[4,4,1024]{2,1,0:T(4,128)(2,1)} %hidden_h.1, s32[4]{0:T(128)} %lengths_h.1, bf16[64,1024]{1,0:T(8,128)(2,1)} %qkv_h.1, bf16[4,128,512]{2,1,0:T(8,128)(2,1)} %keys_h.1, bf16[4,128,512]{2,1,0:T(8,128)(2,1)} %values_h.1, bf16[32,1024]{1,0:T(8,128)(2,1)} %outw_h.1, s32[4,4,8]{2,1,0:T(4,128)} %ids_h.1, ...), custom_call_target="tpu_custom_call" | custom-call | tf_op jit(solution)/shard_map/decoder_layer/pallas_call | solution.py:387
  30.5 0.6 %copy.13 = bf16[4,4,1024]{2,1,0:T(4,128)(2,1)} copy(bf16[4,4,1024]{2,1,0:T(4,128)(2,1)S(1)} %decoder_layer.1) | data formatting | bytes 65536
